TPU v7x, 32 devices: a whole 2x2x4 slice. The times are simulated.
32 devices in a mesh: group: 2 (over y), dp: 16 (over z, x, core).
Axes of the slice: x: 2, y: 2, z: 4, core: 2. Of those that a mesh axis runs over, the one named last changes fastest.
Arguments:
- frames: bfloat16 [2, 64, 128, 84, 336], P('group', 'dp'), may hold values from 0 to 1
- actions: int32 [2, 64, 128], P('group', 'dp'), may hold values from 0 to 17
- rewards: float32 [2, 64, 128], P('group', 'dp'), may hold values from 0 to 0.75
- old_values: float32 [2, 64, 128], P('group', 'dp'), may hold values from -6 to 6
- next_values: float32 [2, 64, 128], P('group', 'dp'), may hold values from -6 to 6
- terminal: int32 [2, 64, 128], P('group', 'dp'), may hold values 0 or 1
- truncated: int32 [2, 64, 128], P('group', 'dp'), may hold values 0 or 1
- behavior_logprob: float32 [2, 64, 128], P('group', 'dp'), may hold values from -3.5 to -2.3
- master: float32 [1695744], P('dp'), may hold values from -2 to 2
- first_moment: float32 [2, 1695744], P('group', 'dp'), may hold values from -1 to 1
- second_moment: float32 [2, 1695744], P('group', 'dp'), may hold values from 0 to 1, as said below
- outer_momentum: float32 [1695744], P('dp'), may hold values from -0.15625 to 0.15625
- step_count: int32 [1], replicated, may hold values from 2 to 20
Outputs:
- grads: float32 [2, 1695744], P('group', 'dp')
- norms: float32 [2], P('group')
- losses: float32 [2], P('group')
- first_new: float32 [2, 1695744], P('group', 'dp')
- second_new: float32 [2, 1695744], P('group', 'dp')
- moved: float32 [1695744], P('dp')
- momentum_new: float32 [1695744], P('dp')
- final: float32 [1695744], P('dp')
- final_low: bfloat16 [1695744], P('dp')
Inputs may be any that keep to these rules, and one draw needn't show every extreme that they name: `second_moment`: entries are positive.
All inputs are finite; a program needn't handle non-finite values. No bound on the sum of `terminal` or of `truncated` on one device may be relied on, other than what follows from the above.
Results may differ from a plain program's by a relative error of at most 0.0011.
The roundings to bfloat16 on the way count: a program that leaves them out, or rounds other values in their place, can miss the bound.
Values may be sent and summed in bfloat16 or wider, within the bound.
No kernel may reach another device: no remote copies, remote signals or barrier semaphores. Data moves between devices by JAX's collectives and lax.ppermute only.
A program may use at most 320 MiB of HBM per device.

v0:
```python
import math
import jax
import jax.numpy as jnp
from jax import lax
from jax.sharding import PartitionSpec as P

C1 = 32
C2 = 64
C3 = 64
HID = 512
ACTIONS = 18
PARAMS = 1693875
BETA_ONE = 0.9
BETA_TWO = 0.999
ADAM_EPSILON = 1e-08
LEARN_RATE = 0.005
WEIGHT_DECAY = 0.01
CLIP_NORM = 0.5
OUTER_RATE = 0.7
OUTER_MOMENTUM = 0.9
DISCOUNT = 0.99
TRACE_DECAY = 0.95
RATIO_CLIP = 0.1
VALUE_COEF = 0.5
ENTROPY_COEF = 0.01


def param_shapes():
    return [
        (8, 8, 4, C1),
        (C1,),
        (4, 4, C1, C2),
        (C2,),
        (3, 3, C2, C3),
        (C3,),
        (49 * C3, HID),
        (HID,),
        (HID, ACTIONS + 1),
        (ACTIONS + 1,),
    ]


def unpack(packed):
    pieces = []
    offset = 0
    for layout in param_shapes():
        length = math.prod(layout)
        pieces.append(packed[offset : offset + length].reshape(layout))
        offset += length
    return pieces


def trajectory_advantages(rewards, values, next_values, terminal, truncated):
    alive = 1.0 - terminal.astype(jnp.float32)
    cutoff = truncated.astype(jnp.float32)
    following = jnp.concatenate([values[:, 1:], next_values[:, -1:]], axis=1)
    following = cutoff * next_values + (1.0 - cutoff) * following
    deltas = rewards + DISCOUNT * alive * following - values
    keeping = DISCOUNT * TRACE_DECAY * alive * (1.0 - cutoff)

    def backward_step(carry, item):
        delta, keep = item
        result = delta + keep * carry
        return (result, result)

    start = jnp.zeros((rewards.shape[0],), jnp.float32)
    _, series = lax.scan(backward_step, start, (deltas.T, keeping.T), reverse=True)
    return series.T


def frame_losses(out, normed, returns, actions, behavior):
    logits = out[:, :ACTIONS]
    value = out[:, ACTIONS]
    log_probs = jax.nn.log_softmax(logits, axis=-1)
    chosen = actions[:, None] == jnp.arange(ACTIONS, dtype=jnp.int32)[None, :]
    taken = jnp.sum(jnp.where(chosen, log_probs, 0.0), axis=-1)
    ratio = jnp.exp(taken - behavior)
    surrogate = jnp.minimum(
        ratio * normed, jnp.clip(ratio, 1.0 - RATIO_CLIP, 1.0 + RATIO_CLIP) * normed
    )
    entropy = -jnp.sum(jnp.exp(log_probs) * log_probs, axis=-1)
    return jnp.sum(-surrogate + 0.5 * VALUE_COEF * (value - returns) ** 2 - ENTROPY_COEF * entropy)


def shifted_conv(inputs, kernel, extent):
    result = 0.0
    for vertical in range(kernel.shape[0]):
        for lateral in range(kernel.shape[1]):
            window = inputs[:, vertical : vertical + extent, lateral : lateral + extent, :]
            result = result + jnp.einsum(
                "bhwc,co->bhwo",
                window,
                kernel[vertical, lateral],
                preferred_element_type=jnp.float32,
            )
    return result


def kernel_grad(inputs, upstream, taps, extent):
    rows_out = []
    for vertical in range(taps):
        line = []
        for lateral in range(taps):
            window = inputs[:, vertical : vertical + extent, lateral : lateral + extent, :]
            line.append(
                jnp.einsum("bhwc,bhwo->co", window, upstream, preferred_element_type=jnp.float32)
            )
        rows_out.append(jnp.stack(line))
    return jnp.stack(rows_out)


def input_grad(upstream, kernel, extent):
    inner_size = upstream.shape[1]
    result = 0.0
    for vertical in range(kernel.shape[0]):
        for lateral in range(kernel.shape[1]):
            term = jnp.einsum(
                "bhwo,co->bhwc",
                upstream,
                kernel[vertical, lateral],
                preferred_element_type=jnp.float32,
            )
            result = result + jnp.pad(
                term,
                (
                    (0, 0),
                    (vertical, extent - inner_size - vertical),
                    (lateral, extent - inner_size - lateral),
                    (0, 0),
                ),
            )
    return result


def column_sum(values):
    return jnp.sum(values.astype(jnp.float32).reshape(-1, values.shape[-1]), axis=0)


def on_device(
    frames,
    actions,
    rewards,
    old_values,
    next_values,
    terminal,
    truncated,
    behavior_logprob,
    master,
    first_moment,
    second_moment,
    outer_momentum,
    step_count,
):
    lanes = lax.axis_size("dp")
    shard_len = master.shape[0]
    weights = lax.all_gather(master.astype(jnp.bfloat16), "dp", axis=0, tiled=True)
    w_one, b_one, w_two, b_two, w_three, b_three, w_dense, b_dense, w_head, b_head = unpack(weights)
    advantage = trajectory_advantages(
        rewards[0], old_values[0], next_values[0], terminal[0], truncated[0]
    )
    envs_here, steps_here = advantage.shape
    batch = envs_here * steps_here
    total_frames = batch * lanes
    first_sum, square_sum = lax.psum((jnp.sum(advantage), jnp.sum(advantage * advantage)), "dp")
    mean = first_sum / total_frames
    spread = square_sum / total_frames - mean * mean
    normed = ((advantage - mean) * lax.rsqrt(spread + 1e-05)).reshape(-1)
    returns = (advantage + old_values[0]).reshape(-1)
    taken_actions = actions[0].reshape(-1)
    behavior = behavior_logprob[0].reshape(-1)
    pixels = (
        frames[0]
        .reshape(batch, 21, 4, 21, 4, 4)
        .transpose(0, 1, 3, 2, 4, 5)
        .reshape(batch, 21, 21, 64)
    )
    kernel_one = w_one.reshape(2, 4, 2, 4, 4, C1).transpose(0, 2, 1, 3, 4, 5).reshape(2, 2, 64, C1)
    conv_one = shifted_conv(pixels, kernel_one, 20) + b_one.astype(jnp.float32)
    act_one = jnp.maximum(conv_one, 0.0).astype(jnp.bfloat16)
    folded_one = (
        act_one.reshape(batch, 10, 2, 10, 2, C1)
        .transpose(0, 1, 3, 2, 4, 5)
        .reshape(batch, 10, 10, 4 * C1)
    )
    kernel_two = (
        w_two.reshape(2, 2, 2, 2, C1, C2).transpose(0, 2, 1, 3, 4, 5).reshape(2, 2, 4 * C1, C2)
    )
    conv_two = shifted_conv(folded_one, kernel_two, 9) + b_two.astype(jnp.float32)
    act_two = jnp.maximum(conv_two, 0.0).astype(jnp.bfloat16)
    conv_three = shifted_conv(act_two, w_three, 7) + b_three.astype(jnp.float32)
    features = jnp.maximum(conv_three, 0.0).astype(jnp.bfloat16).reshape(batch, 49 * C3)
    hidden_pre = jnp.dot(features, w_dense, preferred_element_type=jnp.float32) + b_dense.astype(
        jnp.float32
    )
    hidden = jnp.maximum(hidden_pre, 0.0).astype(jnp.bfloat16)
    out = jnp.dot(hidden, w_head, preferred_element_type=jnp.float32) + b_head.astype(jnp.float32)

    def local_loss(values):
        return frame_losses(values, normed, returns, taken_actions, behavior) / total_frames

    loss_local, pullback = jax.vjp(local_loss, out)
    grad_out = pullback(jnp.ones((), jnp.float32))[0].astype(jnp.bfloat16)
    grad_head = jnp.einsum("bh,bo->ho", hidden, grad_out, preferred_element_type=jnp.float32)
    grad_head_bias = column_sum(grad_out)
    back_hidden = jnp.einsum("bo,ho->bh", grad_out, w_head, preferred_element_type=jnp.float32)
    grad_hidden = jnp.where(hidden_pre > 0, back_hidden, 0.0).astype(jnp.bfloat16)
    grad_dense = jnp.einsum("bi,bh->ih", features, grad_hidden, preferred_element_type=jnp.float32)
    grad_dense_bias = column_sum(grad_hidden)
    back_three = jnp.einsum(
        "bh,ih->bi", grad_hidden, w_dense, preferred_element_type=jnp.float32
    ).reshape(batch, 7, 7, C3)
    grad_conv_three = jnp.where(conv_three > 0, back_three, 0.0).astype(jnp.bfloat16)
    grad_three = kernel_grad(act_two, grad_conv_three, 3, 7)
    grad_three_bias = column_sum(grad_conv_three)
    back_two = input_grad(grad_conv_three, w_three, 9)
    grad_conv_two = jnp.where(conv_two > 0, back_two, 0.0).astype(jnp.bfloat16)
    grad_two_folded = kernel_grad(folded_one, grad_conv_two, 2, 9)
    grad_two = (
        grad_two_folded.reshape(2, 2, 2, 2, C1, C2)
        .transpose(0, 2, 1, 3, 4, 5)
        .reshape(4, 4, C1, C2)
    )
    grad_two_bias = column_sum(grad_conv_two)
    back_folded = input_grad(grad_conv_two, kernel_two, 10)
    back_one = (
        back_folded.reshape(batch, 10, 10, 2, 2, C1)
        .transpose(0, 1, 3, 2, 4, 5)
        .reshape(batch, 20, 20, C1)
    )
    grad_conv_one = jnp.where(conv_one > 0, back_one, 0.0).astype(jnp.bfloat16)
    grad_one_folded = kernel_grad(pixels, grad_conv_one, 2, 20)
    grad_one = (
        grad_one_folded.reshape(2, 2, 4, 4, 4, C1).transpose(0, 2, 1, 3, 4, 5).reshape(8, 8, 4, C1)
    )
    grad_one_bias = column_sum(grad_conv_one)
    pieces = [
        grad_one,
        grad_one_bias,
        grad_two,
        grad_two_bias,
        grad_three,
        grad_three_bias,
        grad_dense,
        grad_dense_bias,
        grad_head,
        grad_head_bias,
    ]
    padding = jnp.zeros((shard_len * lanes - PARAMS,), jnp.float32)
    grad_flat = jnp.concatenate([piece.reshape(-1) for piece in pieces] + [padding])
    summed, loss_total = lax.psum((grad_flat, loss_local), "dp")
    norm = jnp.sqrt(jnp.sum(summed * summed))
    owned = lax.dynamic_slice_in_dim(summed, lax.axis_index("dp") * shard_len, shard_len, 0)
    factor = jnp.minimum(1.0, CLIP_NORM / (norm + 1e-06))
    clipped = owned * factor
    moment_step = step_count[0].astype(jnp.float32)
    first_next = BETA_ONE * first_moment[0] + (1.0 - BETA_ONE) * clipped
    second_next = BETA_TWO * second_moment[0] + (1.0 - BETA_TWO) * clipped * clipped
    first_hat = first_next / (1.0 - jnp.power(BETA_ONE, moment_step))
    second_hat = second_next / (1.0 - jnp.power(BETA_TWO, moment_step))
    inner = master - LEARN_RATE * (
        first_hat / (jnp.sqrt(second_hat) + ADAM_EPSILON) + WEIGHT_DECAY * master
    )
    moved = lax.psum(master - inner, "group") / lax.axis_size("group")
    momentum_next = OUTER_MOMENTUM * outer_momentum + moved
    final = master - OUTER_RATE * (moved + OUTER_MOMENTUM * momentum_next)
    return (
        clipped[None],
        norm.reshape(1),
        loss_total.reshape(1),
        first_next[None],
        second_next[None],
        moved,
        momentum_next,
        final,
        final.astype(jnp.bfloat16),
    )


def solution(mesh):
    return jax.shard_map(
        on_device,
        mesh=mesh,
        in_specs=(
            P("group", "dp", None, None, None),
            P("group", "dp", None),
            P("group", "dp", None),
            P("group", "dp", None),
            P("group", "dp", None),
            P("group", "dp", None),
            P("group", "dp", None),
            P("group", "dp", None),
            P("dp"),
            P("group", "dp"),
            P("group", "dp"),
            P("dp"),
            P(),
        ),
        out_specs=(
            P("group", "dp"),
            P("group"),
            P("group"),
            P("group", "dp"),
            P("group", "dp"),
            P("dp"),
            P("dp"),
            P("dp"),
            P("dp"),
        ),
        check_vma=False,
    )
```

profile of v0, /device:TPU:0, one launch (start us, length us, event | category | flops | bytes accessed | tf_op | source)
XLA Modules:
  0.0 1024.8 jit_solution(7701893610544286102)
XLA Ops:
  11.9 9.6 while.17
  24.1 37.2 %all-reduce.15 = (f32[]{:T(128)}, f32[]{:T(128)}) all-reduce(f32[]{:T(128)} %get-tuple-element.174, f32[]{:T(128)} %reduce_sum.128), channel_id=1, replica_groups=mesh['group'=2,'dp'=16] {'dp'}, use_global_device_ids=true, to_apply=%region_8.9 | all-reduce | flops 2 | bytes 16 | tf_op jit(solution)/shard_map/psum | solution.py:164
  63.9 21.7 %copy.91 = bf16[1,4,128,84,336]{2,1,4,3,0:T(4,128)(2,1)} copy(bf16[1,4,128,84,336]{2,4,3,1,0:T(8,128)(2,1)} %param.15) | data formatting | bytes 57802752 | tf_op args[0]
  85.7 50.5 %reshape_squeeze.8 = bf16[512,21,4,21,4,4]{0,5,4,3,2,1:T(4,128)(2,1)} reshape(bf16[1,4,128,84,336]{2,1,4,3,0:T(4,128)(2,1)} %copy.91) | data formatting | bytes 57802752 | tf_op jit(solution)/shard_map/reshape;squeeze | solution.py:173
  136.1 20.4 %copy.92 = bf16[512,21,21,4,4,4]{0,5,4,3,2,1:T(4,128)(2,1)} copy(bf16[512,21,21,4,4,4]{0,5,4,2,3,1:T(4,128)(2,1)} %bitcast.500) | data formatting | bytes 57802752 | tf_op jit(solution)/shard_map/transpose | solution.py:174
  156.6 45.4 %reshape.158 = bf16[512,21,21,64]{0,3,2,1:T(8,128)(2,1)} reshape(bf16[512,21,21,4,4,4]{0,5,4,3,2,1:T(4,128)(2,1)} %copy.92) | data formatting | bytes 57802752 | tf_op jit(solution)/shard_map/reshape | solution.py:175
  202.0 70.1 %reduce.5 = bf16[16,105984]{1,0:T(8,128)(2,1)S(1)} reduce(bf16[16,1,105984]{2,1,0:T(2,128)(2,1)} %all-gather.3.cloned.1.call-done, bf16[]{:T(256)} %constant.178), dimensions={1}, to_apply=%all-gather.reduce_sub_computation | reduce | bytes 6782978 | tf_op jit(solution)/shard_map/all_gather | solution.py:156
  272.0 6.8 reshape.177
  296.5 19.2 %fusion.4 = f32[512,20,20,32]{0,3,2,1:T(8,128)} fusion(bf16[512,21,21,64]{0,3,2,1:T(8,128)(2,1)} %reshape.158, bf16[2,2,64,32]{3,2,1,0:T(8,128)(2,1)S(1)} %bitcast.516), kind=kOutput, calls=%fused_computation.12 | convolution fusion | flops 838860800 | bytes 52445184 | tf_op jit(solution)/shard_map/bhwc,co->bhwo/dot_general | solution.py:90
  315.7 19.1 %fusion.8 = f32[512,20,20,32]{0,3,2,1:T(8,128)} fusion(bf16[512,21,21,64]{0,3,2,1:T(8,128)(2,1)} %reshape.158, bf16[2,2,64,32]{3,2,1,0:T(8,128)(2,1)S(1)} %bitcast.517), kind=kOutput, calls=%fused_computation.16 | convolution fusion | flops 838860800 | bytes 52445184 | tf_op jit(solution)/shard_map/bhwc,co->bhwo/dot_general | solution.py:90
  334.7 20.3 %fusion.12 = f32[512,20,20,32]{0,3,2,1:T(8,128)} fusion(bf16[512,21,21,64]{0,3,2,1:T(8,128)(2,1)} %reshape.158, bf16[2,2,64,32]{3,2,1,0:T(8,128)(2,1)S(1)} %bitcast.518), kind=kOutput, calls=%fused_computation.20 | convolution fusion | flops 838860800 | bytes 52445184 | tf_op jit(solution)/shard_map/bhwc,co->bhwo/dot_general | solution.py:90
  355.2 46.6 %maximum_convert_fusion = (bf16[512,20,20,32]{0,3,2,1:T(8,128)(2,1)}, f32[512,20,20,32]{0,3,2,1:T(8,128)}) fusion(f32[32]{0:T(128)S(1)} %slice_convert_fusion.4, f32[512,20,20,32]{0,3,2,1:T(8,128)} %fusion.4, f32[512,20,20,32]{0,3,2,1:T(8,128)} %fusion.8, f32[512,20,20,32]{0,3,2,1:T(8,128)} %fusion.12, bf16[512,21,21,64]{0,3,2,1:T(8,128)(2,1)} %reshape.158, ...), kind=kOutput, calls=%fused_computation.8 | convolution fusion | flops 878182400 | bytes 144196096 | tf_op jit(solution)/shard_map/bhwc,co->bhwo/dot_general | solution.py:90
  401.8 6.4 copy.98
  408.2 5.4 fusion.66
  413.6 5.8 fusion.64
  419.4 4.9 fusion.62
  424.4 25.2 %maximum_convert_fusion.1 = (bf16[512,9,9,64]{0,3,2,1:T(8,128)(2,1)}, f32[512,9,9,64]{0,3,2,1:T(8,128)}) fusion(f32[64]{0:T(128)S(1)} %get-tuple-element.168, bf16[512,10,10,128]{0,3,2,1:T(8,128)(2,1)} %bitcast.489, bf16[2,2,128,64]{3,2,1,0:T(8,128)(2,1)S(1)} %bitcast.510, f32[512,9,9,64]{0,3,2,1:T(8,128)} %fusion.66, f32[512,9,9,64]{0,3,2,1:T(8,128)} %fusion.62, ...), kind=kOutput, calls=%fused_computation.30 | convolution fusion | flops 695402496 | bytes 60916224 | tf_op jit(solution)/shard_map/bhwc,co->bhwo/dot_general | solution.py:90
  449.6 5.8 fusion.21
  455.4 3.7 fusion.23
  459.1 3.7 fusion.25
  477.5 3.8 fusion.35
  481.6 18.7 %fusion.41 = (u8[512,7,64]{0,2,1:T(8,128)(4,1)S(1)}, bf16[512,7,7,64]{0,3,2,1:T(8,128)(2,1)S(1)}) fusion(f32[64]{0:T(128)S(1)} %copy-done.39, f32[512,7,7,64]{0,3,2,1:T(8,128)} %fusion.21, f32[512,7,7,64]{0,3,2,1:T(8,128)} %fusion.23, f32[512,7,7,64]{0,3,2,1:T(8,128)} %fusion.25, f32[512,7,7,64]{0,3,2,1:T(8,128)} %fusion.27, f32[512,7,7,64]{0,3,2,1:T(8,128)} %fusion.29, ...), kind=kOutput, calls=%fused_computation.59 | convolution fusion | flops 229376000 | bytes 58049024 | tf_op jit(solution)/shard_map/bhwc,co->bhwo/dot_general | solution.py:90
  525.7 4.5 convolution_bitcast_fusion
  530.3 3.7 fusion.67
  534.0 4.1 fusion.68
  548.9 5.4 fusion.74
  554.3 5.5 fusion.72
  559.8 5.4 fusion.71
  565.2 5.5 fusion.20
  570.7 22.1 %convert_reduce_fusion.2 = (f32[64]{0:T(128)}, bf16[512,9,9,64]{0,3,2,1:T(8,128)(2,1)S(1)}) fusion(bf16[512,7,7,64]{0,3,2,1:T(8,128)(2,1)S(1)} %get-tuple-element.184, bf16[3,3,64,64]{3,2,1,0:T(8,128)(2,1)S(1)} %reshape.163, f32[512,9,9,64]{0,3,2,1:T(8,128)} %fusion.74, f32[512,7,7,64]{0,3,2,1:T(8,128)} %fusion.73, f32[512,9,9,64]{0,3,2,1:T(8,128)} %fusion.72, ...), kind=kOutput, calls=%fused_computation.28 | convolution fusion | flops 247988160 | bytes 73089280 | tf_op jit(solution)/shard_map/jit(_pad)/pad | solution.py:123
  592.8 8.2 fusion.99
  601.0 6.6 fusion.98
  614.7 8.8 fusion.61
  623.5 8.8 fusion.63
  632.3 8.7 fusion.65
  641.0 9.4 convert_reduce_fusion
  650.4 28.9 %add_add_fusion = bf16[512,10,10,128]{0,3,2,1:T(8,128)(2,1)} fusion(f32[512,9,9,128]{0,3,2,1:T(8,128)} %fusion.65, f32[512,9,9,128]{0,3,2,1:T(8,128)} %fusion.63, f32[512,9,9,128]{0,3,2,1:T(8,128)} %fusion.61, bf16[512,9,9,64]{0,3,2,1:T(8,128)(2,1)} %copy-done.1, bf16[2,2,128,64]{3,2,1,0:T(8,128)(2,1)S(1)} %bitcast.514), kind=kOutput, calls=%fused_computation.7 | convolution fusion | flops 705691648 | bytes 82149376 | tf_op jit(solution)/shard_map/jit(_pad)/pad | solution.py:123
  679.3 6.1 copy.129
  685.4 8.3 convert_reduce_fusion.1
  693.7 15.2 %fusion.52 = f32[64,32]{0,1:T(8,128)S(1)} fusion(bf16[512,20,20,32]{0,3,2,1:T(8,128)(2,1)} %get-tuple-element.166, bf16[512,21,21,64]{0,3,2,1:T(8,128)(2,1)} %reshape.158), kind=kOutput, calls=%fused_computation.76 | convolution fusion | flops 838860800 | bytes 39329792 | tf_op jit(solution)/shard_map/bhwc,bhwo->co/dot_general | solution.py:106
  708.9 15.0 %fusion.49 = f32[64,32]{0,1:T(8,128)S(1)} fusion(bf16[512,20,20,32]{0,3,2,1:T(8,128)(2,1)} %get-tuple-element.166, bf16[512,21,21,64]{0,3,2,1:T(8,128)(2,1)} %reshape.158), kind=kOutput, calls=%fused_computation.75 | convolution fusion | flops 838860800 | bytes 39329792 | tf_op jit(solution)/shard_map/bhwc,bhwo->co/dot_general | solution.py:106
  723.9 15.4 %fusion.46 = f32[64,32]{0,1:T(8,128)S(1)} fusion(bf16[512,20,20,32]{0,3,2,1:T(8,128)(2,1)} %get-tuple-element.166, bf16[512,21,21,64]{0,3,2,1:T(8,128)(2,1)} %reshape.158), kind=kOutput, calls=%fused_computation.74 | convolution fusion | flops 838860800 | bytes 39329792 | tf_op jit(solution)/shard_map/bhwc,bhwo->co/dot_general | solution.py:106
  739.4 15.5 %fusion.43 = f32[64,32]{0,1:T(8,128)S(1)} fusion(bf16[512,20,20,32]{0,3,2,1:T(8,128)(2,1)} %get-tuple-element.166, bf16[512,21,21,64]{0,3,2,1:T(8,128)(2,1)} %reshape.158), kind=kOutput, calls=%fused_computation.73 | convolution fusion | flops 838860800 | bytes 39329792 | tf_op jit(solution)/shard_map/bhwc,bhwo->co/dot_general | solution.py:106
  755.5 7.2 copy.220
  763.4 62.0 %concatenate.13 = f32[1695744]{0:T(1024)} concatenate(f32[8192]{0:T(1024)S(1)} %reshape_reshape.14, f32[32]{0:T(128)S(1)} %get-tuple-element.165, f32[32768]{0:T(1024)S(1)} %reshape_reshape.15, f32[64]{0:T(128)S(1)} %copy-done.38, f32[36864]{0:T(1024)S(1)} %reshape.171, f32[64]{0:T(128)S(1)} %copy-done.40, f32[1605632]{0:T(1024)} %bitcast.504, f32[512]{0:T(512)S(1)} %copy-done.30, ...), dimensions={0} | concatenate | bytes 13565952 | tf_op jit(solution)/shard_map/concatenate | solution.py:249
  829.1 140.4 %all-reduce.19.cloned.1.call-done = f32[1695744]{0:T(1024)} async-done(((f32[1695744]{0:T(1024)}), f32[1695744]{0:T(1024)}) %all-reduce.19.cloned.1.call-update) | async-done | bytes 6782992 | tf_op jit(solution)/shard_map/psum | solution.py:250
  969.4 4.5 multiply_reduce_fusion
  978.2 33.3 %psum.38 = f32[1]{0:T(128)} all-reduce(f32[1]{0:T(128)} %bitcast.155), channel_id=1, replica_groups=mesh['group'=2,'dp'=16] {'dp'}, use_global_device_ids=true, to_apply=%region_19.20 | all-reduce | flops 1 | bytes 8 | tf_op jit(solution)/shard_map/psum | solution.py:250
  (454 shorter events, 102.6 us)
Async XLA Ops:
  7.2 194.8 %all-gather.3.cloned.1.call-start = ((), (), s32[]{:S(2)}) async-start(), calls=%async_computation.2 | async-start | bytes 7206912 | tf_op jit(solution)/shard_map/all_gather | solution.py:156
  9.3 960.2 %all-reduce.19.cloned.1.call-start = ((), (), s32[]{:S(2)}) async-start(), calls=%async_computation | async-start | bytes 13565952 | tf_op jit(solution)/shard_map/psum | solution.py:250
  22.2 63.5 %copy-start.24 = (f32[128,4]{0,1:T(4,128)}, f32[128,4]{0,1:T(4,128)S(1)}, u32[]{:S(2)}) copy-start(f32[128,4]{0,1:T(4,128)S(1)} %copy.119) | copy-start | bytes 6148
  289.8 6.6 slice-start.8
  408.2 11.2 %copy-start = (bf16[512,10,2,10,2,32]{0,5,4,2,3,1:T(8,128)(2,1)}, bf16[512,10,2,10,2,32]{0,5,4,2,3,1:T(8,128)(2,1)S(1)}, u32[]{:S(2)}) copy-start(bf16[512,10,2,10,2,32]{0,5,4,2,3,1:T(8,128)(2,1)S(1)} %copy.98) | copy-start | bytes 39321604
  449.6 5.8 slice-start.4
  449.6 5.8 slice-start.5
  477.5 3.8 copy-start.22
  477.5 4.1 copy-start.39
  502.3 2.3 copy-start.35
  502.3 2.9 copy-start.27
  502.3 3.0 copy-start.25
  502.3 3.0 copy-start.32
  502.3 6.3 copy-start.3
  506.6 4.9 slice-start.6
  508.6 2.9 slice-start.7
  592.8 39.5 %copy-start.1 = (bf16[512,9,9,64]{0,3,2,1:T(8,128)(2,1)}, bf16[512,9,9,64]{0,3,2,1:T(8,128)(2,1)S(1)}, u32[]{:S(2)}) copy-start(bf16[512,9,9,64]{0,3,2,1:T(8,128)(2,1)S(1)} %get-tuple-element.182) | copy-start | bytes 15925252
  592.8 14.8 %slice-start = ((s8[13107200]{0:T(1024)(128)(4,1)}), s8[4194304]{0:T(1024)(128)(4,1)S(1)}, s32[]{:S(2)}) async-start(s8[13107200]{0:T(1024)(128)(4,1)} %bitcast.492), calls=%async_computation.3 | async-start | bytes 8388608
  592.8 14.8 %slice-start.1 = ((s8[13107200]{0:T(1024)(128)(4,1)}), s8[4194304]{0:T(1024)(128)(4,1)S(1)}, s32[]{:S(2)}) async-start(s8[13107200]{0:T(1024)(128)(4,1)} %bitcast.492), calls=%async_computation.4 | async-start | bytes 8388608
  601.0 6.6 slice-start.2
  601.0 6.6 slice-start.3
  739.3 15.6 %copy-start.5 = (f32[512,19]{1,0:T(8,128)S(1)}, f32[512,19]{1,0:T(8,128)}, u32[]{:S(2)}) copy-start(f32[512,19]{1,0:T(8,128)} %fusion.57) | copy-start | bytes 116740
  739.3 15.8 %copy-start.19 = (f32[1,64,64]{2,1,0:T(8,128)S(1)}, f32[1,64,64]{2,1,0:T(8,128)}, u32[]{:S(2)}) copy-start(f32[1,64,64]{2,1,0:T(8,128)} %convolution_bitcast_fusion.1) | copy-start | bytes 49156
  739.3 15.8 %copy-start.20 = (f32[1,64,64]{2,1,0:T(8,128)S(1)}, f32[1,64,64]{2,1,0:T(8,128)}, u32[]{:S(2)}) copy-start(f32[1,64,64]{2,1,0:T(8,128)} %convolution_bitcast_fusion.2) | copy-start | bytes 49156
  739.3 15.8 %copy-start.21 = (f32[1,64,64]{2,1,0:T(8,128)S(1)}, f32[1,64,64]{2,1,0:T(8,128)}, u32[]{:S(2)}) copy-start(f32[1,64,64]{2,1,0:T(8,128)} %convolution_bitcast_fusion.3) | copy-start | bytes 49156
  739.3 15.8 %copy-start.13 = (f32[1,64,64]{2,1,0:T(8,128)S(1)}, f32[1,64,64]{2,1,0:T(8,128)}, u32[]{:S(2)}) copy-start(f32[1,64,64]{2,1,0:T(8,128)} %convolution_bitcast_fusion.4) | copy-start | bytes 49156
  739.4 15.8 %copy-start.14 = (f32[1,64,64]{2,1,0:T(8,128)S(1)}, f32[1,64,64]{2,1,0:T(8,128)}, u32[]{:S(2)}) copy-start(f32[1,64,64]{2,1,0:T(8,128)} %convolution_bitcast_fusion.5) | copy-start | bytes 49156
  739.4 15.8 %copy-start.15 = (f32[1,64,64]{2,1,0:T(8,128)S(1)}, f32[1,64,64]{2,1,0:T(8,128)}, u32[]{:S(2)}) copy-start(f32[1,64,64]{2,1,0:T(8,128)} %convolution_bitcast_fusion.6) | copy-start | bytes 49156
  739.4 15.8 %copy-start.16 = (f32[1,64,64]{2,1,0:T(8,128)S(1)}, f32[1,64,64]{2,1,0:T(8,128)}, u32[]{:S(2)}) copy-start(f32[1,64,64]{2,1,0:T(8,128)} %convolution_bitcast_fusion.7) | copy-start | bytes 49156
  739.4 15.8 %copy-start.17 = (f32[1,64,64]{2,1,0:T(8,128)S(1)}, f32[1,64,64]{2,1,0:T(8,128)}, u32[]{:S(2)}) copy-start(f32[1,64,64]{2,1,0:T(8,128)} %convolution_bitcast_fusion.8) | copy-start | bytes 49156
  739.4 15.8 %copy-start.18 = (f32[1,64,64]{2,1,0:T(8,128)S(1)}, f32[1,64,64]{2,1,0:T(8,128)}, u32[]{:S(2)}) copy-start(f32[1,64,64]{2,1,0:T(8,128)} %convolution_bitcast_fusion.9) | copy-start | bytes 49156
  755.4 7.3 copy-start.9
  755.4 7.3 copy-start.10
  755.4 7.3 copy-start.11
  755.4 7.3 copy-start.12
  755.4 7.9 copy-start.30
  755.4 7.9 copy-start.36
  755.5 7.9 copy-start.38
  755.5 7.9 copy-start.40
  825.4 149.2 %copy-start.2 = (f32[105984]{0:T(1024)S(1)}, f32[105984]{0:T(1024)}, u32[]{:S(2)}) copy-start(f32[105984]{0:T(1024)} %param.23) | copy-start | bytes 1271812
  825.5 151.4 %copy-start.23 = (f32[1,4,128]{2,1,0:T(4,128)S(1)}, f32[1,4,128]{2,1,0:T(4,128)}, u32[]{:S(2)}) copy-start(f32[1,4,128]{2,1,0:T(4,128)} %param.18) | copy-start | bytes 6148
  825.5 151.4 %copy-start.26 = (f32[128,4]{0,1:T(4,128)S(1)}, f32[128,4]{0,1:T(4,128)}, u32[]{:S(2)}) copy-start(f32[128,4]{0,1:T(4,128)} %copy-done.24) | copy-start | bytes 6148
  825.5 151.4 %copy-start.29 = (f32[512]{0:T(512)S(1)}, f32[512]{0:T(512)}, u32[]{:S(2)}) copy-start(f32[512]{0:T(512)} %copy-done.28) | copy-start | bytes 6148
  825.5 151.4 %copy-start.31 = (f32[512]{0:T(512)S(1)}, f32[512]{0:T(512)}, u32[]{:S(2)}) copy-start(f32[512]{0:T(512)} %get-tuple-element.141) | copy-start | bytes 6148
  825.5 151.4 %copy-start.33 = (f32[1,4,128]{2,1,0:T(4,128)S(1)}, f32[1,4,128]{2,1,0:T(4,128)}, u32[]{:S(2)}) copy-start(f32[1,4,128]{2,1,0:T(4,128)} %param.22) | copy-start | bytes 6148
  825.5 151.4 %copy-start.34 = (f32[512,1]{0,1:T(1,128)S(1)}, f32[512,1]{0,1:T(1,128)}, u32[]{:S(2)}) copy-start(f32[512,1]{0,1:T(1,128)} %get-tuple-element.169) | copy-start | bytes 6148
  825.5 189.1 %all-reduce.21.cloned.1.call-start = ((), (), s32[]{:S(2)}) async-start(), calls=%async_computation.1 | async-start | bytes 851968 | tf_op jit(solution)/shard_map/psum | solution.py:263
  829.1 185.6 %copy-start.6 = (f32[105984]{0:T(1024)S(1)}, f32[105984]{0:T(1024)}, u32[]{:S(2)}) copy-start(f32[105984]{0:T(1024)} %param.26) | copy-start | bytes 1271812
  (6 other events, 8.6 us)
Sparse Core Ops, SparseCore 0:
  10.7 67.2 all-gather.2
  825.6 143.8 all-reduce.18
  977.0 26.5 all-reduce.20
where the time goes:
time: 1040 us; the launch traced here: 1020 us
  matrix products  418 us (40%)
  local copies, waits for them, and re-layouts  253 us (24%)
  waiting for transfers between devices  140 us (13%)
  other arithmetic  119 us (11%)
  blocking collectives  70.6 us (7%)
  between operations  20.8 us (2%)
    dot_general x17, matrix products, shifted_conv(): jnp.einsum('bhwc,co->bhwo', window, kernel[vertical, lateral], preferred_...  197 us
    psum x1, waiting for transfers between devices, on_device(): summed, loss_total = lax.psum((grad_flat, loss_local), 'dp')  140 us
    dot_general x17, matrix products, kernel_grad(): jnp.einsum('bhwc,bhwo->co', window, upstream, preferred_element_type=jnp....  97.1 us
    all_gather x1, other arithmetic, on_device(): lax.all_gather(master.astype(jnp.bfloat16), 'dp', axis=0, tiled=True)  70.1 us
    pad x5, matrix products, input_grad(): jnp.pad(term, ((0, 0), (vertical, extent - inner_size - vertical), (later...  67.2 us
    concatenate x1, local copies, waits for them, and re-layouts, on_device(): jnp.concatenate([piece.reshape(-1) for piece in pieces] + [padding])  62 us
    another operation x1, local copies, waits for them, and re-layouts, on_device(): pixels = frames[0].reshape(batch, 21, 4, 21, 4, 4).transpose(0, 1, 3, 2,...  50.5 us
    reshape x1, local copies, waits for them, and re-layouts, on_device(): pixels = frames[0].reshape(batch, 21, 4, 21, 4, 4).transpose(0, 1, 3, 2,...  45.4 us
  transfers between devices with their start and end apart: 3, of which 1 were waited for; matrix products, arithmetic and copies ran while one was open for 15% of the time, Pallas kernels for 0%

commit v1 on v0

--- a/solution.py
+++ b/solution.py
@@ -23,6 +23,18 @@
 RATIO_CLIP = 0.1
 VALUE_COEF = 0.5
 ENTROPY_COEF = 0.01
+
+
+def collect(shard, axis, dim):
+    ways, here = (lax.axis_size(axis), lax.axis_index(axis))
+    grown, reach = (shard, 1)
+    while reach < ways:
+        theirs = lax.ppermute(grown, axis, [(d, d ^ reach) for d in range(ways)])
+        mine_first = jnp.concatenate([grown, theirs], axis=dim)
+        theirs_first = jnp.concatenate([theirs, grown], axis=dim)
+        grown = jnp.where(here & reach == 0, mine_first, theirs_first)
+        reach = 2 * reach
+    return grown
 
 
 def param_shapes():
@@ -153,7 +165,7 @@
 ):
     lanes = lax.axis_size("dp")
     shard_len = master.shape[0]
-    weights = lax.all_gather(master.astype(jnp.bfloat16), "dp", axis=0, tiled=True)
+    weights = collect(master.astype(jnp.bfloat16), "dp", 0)
     w_one, b_one, w_two, b_two, w_three, b_three, w_dense, b_dense, w_head, b_head = unpack(weights)
     advantage = trajectory_advantages(
         rewards[0], old_values[0], next_values[0], terminal[0], truncated[0]

time: 1040 us -> 1130 us (1.087)
  other arithmetic: 119 us -> 147 us
  local copies, waits for them, and re-layouts: 253 us -> 281 us
  waiting for transfers between devices: 140 us -> 167 us
    add x128, other arithmetic: 2.43 us -> 90.3 us  [backward_step(): result = delta + keep * carry]
    all_gather x1 -> x0, other arithmetic: 70.1 us -> none  [on_device(): lax.all_gather(master.astype(jnp.bfloat16), 'dp', axis=0, tiled=True)]
    ppermute x0 -> x4, waiting for transfers between devices: none -> 26.5 us  [collect(): theirs = lax.ppermute(grown, axis, [(d, d ^ reach) for d in range(ways)])]
    concatenate x0 -> x2, local copies, waits for them, and re-layouts: none -> 22.4 us  [collect(): mine_first = jnp.concatenate([grown, theirs], axis=dim)]
    select_n x0 -> x2, local copies, waits for them, and re-layouts: none -> 17.2 us  [collect(): grown = jnp.where(here & reach == 0, mine_first, theirs_first)]
    select_n x0 -> x4, other arithmetic: none -> 12.6 us  [collect(): grown = jnp.where(here & reach == 0, mine_first, theirs_first)]
    unnamed x106 -> x108, local copies, waits for them, and re-layouts: 38.4 us -> 31.4 us
  transfers between devices with their start and end apart: 3 -> 6, of which waited for: 1 -> 4; matrix products, arithmetic and copies ran while one was open for 15% -> 23% of each run, Pallas kernels for 0% -> 0%
where the time goes in v1:
time: 1130 us; the launch traced here: 1110 us
  matrix products  417 us (37%)
  local copies, waits for them, and re-layouts  281 us (25%)
  waiting for transfers between devices  167 us (15%)
  other arithmetic  147 us (13%)
  blocking collectives  63.5 us (6%)
  between operations  21.2 us (2%)
    dot_general x17, matrix products, shifted_conv(): jnp.einsum('bhwc,co->bhwo', window, kernel[vertical, lateral], preferred_...  197 us
    psum x1, waiting for transfers between devices, on_device(): summed, loss_total = lax.psum((grad_flat, loss_local), 'dp')  140 us
    dot_general x17, matrix products, kernel_grad(): jnp.einsum('bhwc,bhwo->co', window, upstream, preferred_element_type=jnp....  96.4 us
    add x128, other arithmetic, backward_step(): result = delta + keep * carry  90.3 us
    pad x5, matrix products, input_grad(): jnp.pad(term, ((0, 0), (vertical, extent - inner_size - vertical), (later...  67.2 us
    concatenate x1, local copies, waits for them, and re-layouts, on_device(): jnp.concatenate([piece.reshape(-1) for piece in pieces] + [padding])  62.3 us
    another operation x1, local copies, waits for them, and re-layouts, on_device(): pixels = frames[0].reshape(batch, 21, 4, 21, 4, 4).transpose(0, 1, 3, 2,...  50.5 us
    reshape x1, local copies, waits for them, and re-layouts, on_device(): pixels = frames[0].reshape(batch, 21, 4, 21, 4, 4).transpose(0, 1, 3, 2,...  45.4 us
  transfers between devices with their start and end apart: 6, of which 4 were waited for; matrix products, arithmetic and copies ran while one was open for 23% of the time, Pallas kernels for 0%

profile of v1, /device:TPU:0, one launch (start us, length us, event | category | flops | bytes accessed | tf_op | source)
XLA Modules:
  0.0 1105.9 jit_solution(8843107259524715852)
XLA Ops:
  13.0 10.1 collective-permute-done.1
  28.3 15.3 %collective-permute-done.2 = bf16[423936]{0:T(1024)(128)(2,1)S(1)} collective-permute-done((bf16[423936]{0:T(1024)(128)(2,1)S(1)}, bf16[423936]{0:T(1024)(128)(2,1)S(1)}, u32[]{:S(2)}, u32[]{:S(2)}) %collective-permute-start.2) | collective-permute-done | bytes 847904 | tf_op jit(solution)/shard_map/ppermute | solution.py:32
  46.8 94.4 %while.17 = (s32[]{:T(128)}, f32[4]{0:T(128)S(1)}, f32[128,4]{1,0:T(8,128)S(1)}, f32[128,4]{1,0:T(8,128)}, f32[128,4]{1,0:T(8,128)S(1)}, /*index=5*/s32[]{:T(128)}, s32[]{:T(128)}, s32[]{:T(128)}) while((s32[]{:T(128)}, f32[4]{0:T(128)S(1)}, f32[128,4]{1,0:T(8,128)S(1)}, f32[128,4]{1,0:T(8,128)}, f32[128,4]{1,0:T(8,128)S(1)}, ...), condition=%wide.region_1.2_spmd.clone, body=%wide.region_0.1_spmd.clone.sunk | while | flops 16 | bytes 219 | solution.py:79
  143.0 30.1 %all-reduce.15 = (f32[]{:T(128)}, f32[]{:T(128)}) all-reduce(f32[]{:T(128)} %get-tuple-element.174, f32[]{:T(128)} %reduce_sum.128), channel_id=1, replica_groups=mesh['group'=2,'dp'=16] {'dp'}, use_global_device_ids=true, to_apply=%region_8.9 | all-reduce | flops 2 | bytes 16 | tf_op jit(solution)/shard_map/psum | solution.py:176
  175.8 21.7 %copy.97 = bf16[1,4,128,84,336]{2,1,4,3,0:T(4,128)(2,1)} copy(bf16[1,4,128,84,336]{2,4,3,1,0:T(8,128)(2,1)} %param.15) | data formatting | bytes 57802752 | tf_op args[0]
  197.5 50.5 %reshape_squeeze.8 = bf16[512,21,4,21,4,4]{0,5,4,3,2,1:T(4,128)(2,1)} reshape(bf16[1,4,128,84,336]{2,1,4,3,0:T(4,128)(2,1)} %copy.97) | data formatting | bytes 57802752 | tf_op jit(solution)/shard_map/reshape;squeeze | solution.py:185
  248.0 20.2 %copy.98 = bf16[512,21,21,4,4,4]{0,5,4,3,2,1:T(4,128)(2,1)} copy(bf16[512,21,21,4,4,4]{0,5,4,2,3,1:T(4,128)(2,1)} %bitcast.508) | data formatting | bytes 57802752 | tf_op jit(solution)/shard_map/transpose | solution.py:186
  268.1 45.4 %reshape.160 = bf16[512,21,21,64]{0,3,2,1:T(8,128)(2,1)} reshape(bf16[512,21,21,4,4,4]{0,5,4,3,2,1:T(4,128)(2,1)} %copy.98) | data formatting | bytes 57802752 | tf_op jit(solution)/shard_map/reshape | solution.py:187
  313.5 4.9 select_n.103
  318.5 12.2 %copy.91 = bf16[207,4,2,4,4,32]{0,5,4,3,2,1:T(8,128)(2,1)} copy(bf16[207,4,2,4,4,32]{5,4,3,2,1,0:T(4,128)(2,1)} %select_n.103) | data formatting | bytes 3391488 | tf_op jit(solution)/shard_map/jit(_where)/select_n | solution.py:35
  330.7 11.8 %maximum_select_fusion = bf16[1695744]{0:T(1024)(128)(2,1)S(1)} fusion(bf16[847872]{0:T(1024)(128)(2,1)S(1)} %collective-permute-done.3, bf16[847872]{0:T(1024)(128)(2,1)S(1)} %maximum_select_fusion.1, pred[]{:T(512)S(6)} %eq.45), kind=kLoop, calls=%fused_computation.38 | loop fusion | flops 15261696 | bytes 6782977 | tf_op jit(solution)/shard_map/jit(_where)/select_n | solution.py:35
  353.6 10.0 concatenate.50
  363.6 12.4 %copy.92 = bf16[207,4,2,4,4,32]{0,5,4,3,2,1:T(8,128)(2,1)} copy(bf16[207,4,2,4,4,32]{5,4,3,2,1,0:T(4,128)(2,1)} %concatenate.50) | data formatting | bytes 3391488 | tf_op jit(solution)/shard_map/concatenate | solution.py:33
  378.4 19.0 %fusion.4 = f32[32,512,20,20]{1,0,3,2:T(8,128)} fusion(bf16[512,21,21,64]{0,3,2,1:T(8,128)(2,1)} %reshape.160, bf16[2,2,64,32]{3,2,1,0:T(8,128)(2,1)S(1)} %bitcast.524), kind=kOutput, calls=%fused_computation.10 | convolution fusion | flops 838860800 | bytes 52445184 | tf_op jit(solution)/shard_map/bhwc,co->bhwo/dot_general | solution.py:102
  397.4 19.1 %fusion.8 = f32[32,512,20,20]{1,0,3,2:T(8,128)} fusion(bf16[512,21,21,64]{0,3,2,1:T(8,128)(2,1)} %reshape.160, bf16[2,2,64,32]{3,2,1,0:T(8,128)(2,1)S(1)} %bitcast.525), kind=kOutput, calls=%fused_computation.14 | convolution fusion | flops 838860800 | bytes 52445184 | tf_op jit(solution)/shard_map/bhwc,co->bhwo/dot_general | solution.py:102
  416.5 20.1 %fusion.12 = f32[32,512,20,20]{1,0,3,2:T(8,128)} fusion(bf16[512,21,21,64]{0,3,2,1:T(8,128)(2,1)} %reshape.160, bf16[2,2,64,32]{3,2,1,0:T(8,128)(2,1)S(1)} %bitcast.526), kind=kOutput, calls=%fused_computation.18 | convolution fusion | flops 838860800 | bytes 52445184 | tf_op jit(solution)/shard_map/bhwc,co->bhwo/dot_general | solution.py:102
  436.8 46.4 %maximum_convert_fusion = (bf16[32,512,20,20]{1,0,3,2:T(8,128)(2,1)}, f32[32,512,20,20]{1,0,3,2:T(8,128)}) fusion(f32[32]{0:T(128)S(1)} %slice_convert_fusion.4, f32[32,512,20,20]{1,0,3,2:T(8,128)} %fusion.4, f32[32,512,20,20]{1,0,3,2:T(8,128)} %fusion.8, f32[32,512,20,20]{1,0,3,2:T(8,128)} %fusion.12, bf16[512,21,21,64]{0,3,2,1:T(8,128)(2,1)} %reshape.160, ...), kind=kOutput, calls=%fused_computation.3 | convolution fusion | flops 878182400 | bytes 144196096 | tf_op jit(solution)/shard_map/bhwc,co->bhwo/dot_general | solution.py:102
  483.2 6.4 copy.102
  489.6 5.3 fusion.66
  494.9 5.7 fusion.64
  500.7 5.3 fusion.62
  506.1 25.0 %maximum_convert_fusion.1 = (bf16[512,9,9,64]{0,3,2,1:T(8,128)(2,1)}, f32[512,9,9,64]{0,3,2,1:T(8,128)}) fusion(f32[64]{0:T(128)S(1)} %get-tuple-element.168, bf16[512,10,10,128]{0,3,2,1:T(8,128)(2,1)} %bitcast.497, bf16[2,2,128,64]{3,2,1,0:T(8,128)(2,1)S(1)} %bitcast.518, f32[512,9,9,64]{0,3,2,1:T(8,128)} %fusion.66, f32[512,9,9,64]{0,3,2,1:T(8,128)} %fusion.62, ...), kind=kOutput, calls=%fused_computation.28 | convolution fusion | flops 695402496 | bytes 60916224 | tf_op jit(solution)/shard_map/bhwc,co->bhwo/dot_general | solution.py:102
  531.2 5.8 fusion.23
  563.4 18.7 %fusion.39 = (u8[512,7,64]{0,2,1:T(8,128)(4,1)S(1)}, bf16[512,7,7,64]{0,3,2,1:T(8,128)(2,1)S(1)}) fusion(f32[64]{0:T(128)S(1)} %copy-done.41, bf16[512,9,9,64]{0,3,2,1:T(8,128)(2,1)} %get-tuple-element.177, bf16[3,3,64,64]{3,2,1,0:T(8,128)(2,1)S(1)} %reshape.164, f32[512,7,7,64]{0,3,2,1:T(8,128)} %fusion.23, f32[512,7,7,64]{0,3,2,1:T(8,128)} %fusion.25, ...), kind=kOutput, calls=%fused_computation.59 | convolution fusion | flops 229376000 | bytes 58049024 | tf_op jit(solution)/shard_map/bhwc,co->bhwo/dot_general | solution.py:102
  607.4 4.6 convolution_bitcast_fusion
  615.6 4.1 fusion.68
  630.6 5.5 fusion.74
  636.1 5.5 fusion.72
  641.6 5.5 fusion.71
  647.1 5.5 fusion.20
  652.6 22.0 %convert_reduce_fusion.1 = (f32[64]{0:T(128)}, bf16[512,9,9,64]{0,3,2,1:T(8,128)(2,1)S(1)}) fusion(bf16[512,7,7,64]{0,3,2,1:T(8,128)(2,1)S(1)} %get-tuple-element.184, bf16[3,3,64,64]{3,2,1,0:T(8,128)(2,1)S(1)} %reshape.164, f32[512,9,9,64]{0,3,2,1:T(8,128)} %fusion.74, f32[512,7,7,64]{0,3,2,1:T(8,128)} %fusion.73, f32[512,9,9,64]{0,3,2,1:T(8,128)} %fusion.72, ...), kind=kOutput, calls=%fused_computation.26 | convolution fusion | flops 247988160 | bytes 73089280 | tf_op jit(solution)/shard_map/jit(_pad)/pad | solution.py:135
  674.7 8.2 fusion.101
  682.9 6.6 fusion.100
  695.9 8.8 fusion.61
  704.7 8.8 fusion.63
  713.5 8.8 fusion.65
  722.3 28.6 %add_add_fusion = bf16[512,10,10,128]{0,3,2,1:T(8,128)(2,1)} fusion(f32[512,9,9,128]{0,3,2,1:T(8,128)} %fusion.65, f32[512,9,9,128]{0,3,2,1:T(8,128)} %fusion.63, f32[512,9,9,128]{0,3,2,1:T(8,128)} %fusion.61, bf16[512,9,9,64]{0,3,2,1:T(8,128)(2,1)} %copy-done.1, bf16[2,2,128,64]{3,2,1,0:T(8,128)(2,1)S(1)} %bitcast.522), kind=kOutput, calls=%fused_computation.6 | convolution fusion | flops 705691648 | bytes 82149376 | tf_op jit(solution)/shard_map/jit(_pad)/pad | solution.py:135
  750.9 6.1 copy.133
  757.1 16.9 %convert_reduce_fusion = (f32[32]{0:T(128)S(1)}, bf16[512,20,20,32]{0,3,2,1:T(8,128)(2,1)}) fusion(bf16[512,20,20,32]{0,3,2,1:T(8,128)(2,1)S(1)} %bitcast.511, f32[32,512,20,20]{1,0,3,2:T(8,128)} %get-tuple-element.176), kind=kLoop, calls=%fused_computation.4 | loop fusion | flops 26214368 | bytes 52428928 | tf_op jit(solution)/shard_map/reduce_sum | solution.py:148
  774.0 15.0 %fusion.50 = f32[64,32]{0,1:T(8,128)S(1)} fusion(bf16[512,20,20,32]{0,3,2,1:T(8,128)(2,1)} %get-tuple-element.166, bf16[512,21,21,64]{0,3,2,1:T(8,128)(2,1)} %reshape.160), kind=kOutput, calls=%fused_computation.76 | convolution fusion | flops 838860800 | bytes 39329792 | tf_op jit(solution)/shard_map/bhwc,bhwo->co/dot_general | solution.py:118
  789.0 15.2 %fusion.47 = f32[64,32]{0,1:T(8,128)S(1)} fusion(bf16[512,20,20,32]{0,3,2,1:T(8,128)(2,1)} %get-tuple-element.166, bf16[512,21,21,64]{0,3,2,1:T(8,128)(2,1)} %reshape.160), kind=kOutput, calls=%fused_computation.75 | convolution fusion | flops 838860800 | bytes 39329792 | tf_op jit(solution)/shard_map/bhwc,bhwo->co/dot_general | solution.py:118
  804.2 15.4 %fusion.44 = f32[64,32]{0,1:T(8,128)S(1)} fusion(bf16[512,20,20,32]{0,3,2,1:T(8,128)(2,1)} %get-tuple-element.166, bf16[512,21,21,64]{0,3,2,1:T(8,128)(2,1)} %reshape.160), kind=kOutput, calls=%fused_computation.74 | convolution fusion | flops 838860800 | bytes 39329792 | tf_op jit(solution)/shard_map/bhwc,bhwo->co/dot_general | solution.py:118
  819.7 15.5 %fusion.41 = f32[64,32]{0,1:T(8,128)S(1)} fusion(bf16[512,20,20,32]{0,3,2,1:T(8,128)(2,1)} %get-tuple-element.166, bf16[512,21,21,64]{0,3,2,1:T(8,128)(2,1)} %reshape.160), kind=kOutput, calls=%fused_computation.73 | convolution fusion | flops 838860800 | bytes 39329792 | tf_op jit(solution)/shard_map/bhwc,bhwo->co/dot_general | solution.py:118
  835.8 7.3 copy.224
  843.8 62.3 %concatenate.56 = f32[1695744]{0:T(1024)} concatenate(f32[8192]{0:T(1024)S(1)} %reshape_reshape.11, f32[32]{0:T(128)S(1)} %get-tuple-element.165, f32[32768]{0:T(1024)S(1)} %reshape_reshape.12, f32[64]{0:T(128)S(1)} %copy-done.40, f32[36864]{0:T(1024)S(1)} %reshape.172, f32[64]{0:T(128)S(1)} %copy-done.42, f32[1605632]{0:T(1024)} %bitcast.512, f32[512]{0:T(512)S(1)} %copy-done.32, ...), dimensions={0} | concatenate | bytes 13565952 | tf_op jit(solution)/shard_map/concatenate | solution.py:261
  909.7 140.4 %all-reduce.19.cloned.1.call-done = f32[1695744]{0:T(1024)} async-done(((f32[1695744]{0:T(1024)}), f32[1695744]{0:T(1024)}) %all-reduce.19.cloned.1.call-update) | async-done | bytes 6782992 | tf_op jit(solution)/shard_map/psum | solution.py:262
  1050.1 4.5 multiply_reduce_fusion
  1058.9 33.3 %psum.38 = f32[1]{0:T(128)} all-reduce(f32[1]{0:T(128)} %bitcast.157), channel_id=1, replica_groups=mesh['group'=2,'dp'=16] {'dp'}, use_global_device_ids=true, to_apply=%region_19.20 | all-reduce | flops 1 | bytes 8 | tf_op jit(solution)/shard_map/psum | solution.py:262
  (465 shorter events, 207.9 us)
Async XLA Ops:
  7.2 134.6 %copy-start.24 = (f32[1,4,128]{2,1,0:T(4,128)S(1)}, f32[1,4,128]{2,1,0:T(4,128)}, u32[]{:S(2)}) copy-start(f32[1,4,128]{2,1,0:T(4,128)} %param.18) | copy-start | bytes 6148
  7.2 1043.0 %all-reduce.19.cloned.1.call-start = ((), (), s32[]{:S(2)}) async-start(), calls=%async_computation | async-start | bytes 13565952 | tf_op jit(solution)/shard_map/psum | solution.py:262
  8.3 1.6 collective-permute-start
  10.1 13.0 %collective-permute-start.1 = (bf16[211968]{0:T(1024)(128)(2,1)S(1)}, bf16[211968]{0:T(1024)(128)(2,1)S(1)}, u32[]{:S(2)}, u32[]{:S(2)}) collective-permute-start(bf16[211968]{0:T(1024)(128)(2,1)S(1)} %maximum_select_fusion.3), channel_id=1, source_target_pairs={{0,2},{1,3},{2,0},{3,1},{4,6},{5,7},{6,4},{7,5},{8,10},{9,11},{10,... | collective-permute-start | bytes 1271816 | tf_op jit(solution)/shard_map/ppermute | solution.py:32
  23.3 20.4 %collective-permute-start.2 = (bf16[423936]{0:T(1024)(128)(2,1)S(1)}, bf16[423936]{0:T(1024)(128)(2,1)S(1)}, u32[]{:S(2)}, u32[]{:S(2)}) collective-permute-start(bf16[423936]{0:T(1024)(128)(2,1)S(1)} %maximum_select_fusion.2), channel_id=1, source_target_pairs={{0,4},{1,5},{2,6},{3,7},{4,0},{5,1},{6,2},{7,3},{8,12},{9,13},{10,... | collective-permute-start | bytes 2543624 | tf_op jit(solution)/shard_map/ppermute | solution.py:32
  44.1 286.6 %collective-permute-start.3 = (bf16[847872]{0:T(1024)(128)(2,1)S(1)}, bf16[847872]{0:T(1024)(128)(2,1)S(1)}, u32[]{:S(2)}, u32[]{:S(2)}) collective-permute-start(bf16[847872]{0:T(1024)(128)(2,1)S(1)} %maximum_select_fusion.1), channel_id=1, source_target_pairs={{0,8},{1,9},{2,10},{3,11},{4,12},{5,13},{6,14},{7,15},{8,0},{9,1},... | collective-permute-start | bytes 5087240 | tf_op jit(solution)/shard_map/ppermute | solution.py:32
  141.8 55.7 %copy-start.26 = (f32[128,4]{0,1:T(4,128)}, f32[128,4]{0,1:T(4,128)S(1)}, u32[]{:S(2)}) copy-start(f32[128,4]{0,1:T(4,128)S(1)} %copy.123) | copy-start | bytes 6148
  330.7 14.4 %copy-start.3 = (bf16[847872]{0:T(1024)(128)(2,1)}, bf16[847872]{0:T(1024)(128)(2,1)S(1)}, u32[]{:S(2)}) copy-start(bf16[847872]{0:T(1024)(128)(2,1)S(1)} %collective-permute-done.3) | copy-start | bytes 5087236
  363.6 12.4 %copy-start.2 = (bf16[207,4,2,4,4,32]{0,5,4,3,2,1:T(8,128)(2,1)S(1)}, bf16[207,4,2,4,4,32]{0,5,4,3,2,1:T(8,128)(2,1)}, u32[]{:S(2)}) copy-start(bf16[207,4,2,4,4,32]{0,5,4,3,2,1:T(8,128)(2,1)} %copy.91) | copy-start | bytes 5087236
  489.6 11.1 %copy-start = (bf16[512,10,2,10,2,32]{0,5,4,2,3,1:T(8,128)(2,1)}, bf16[512,10,2,10,2,32]{0,5,4,2,3,1:T(8,128)(2,1)S(1)}, u32[]{:S(2)}) copy-start(bf16[512,10,2,10,2,32]{0,5,4,2,3,1:T(8,128)(2,1)S(1)} %copy.102) | copy-start | bytes 39321604
  531.2 5.8 slice-start.4
  531.2 5.8 slice-start.5
  559.3 3.9 copy-start.23
  559.3 4.1 copy-start.41
  584.0 2.9 copy-start.27
  584.1 6.2 copy-start.5
  588.3 4.9 slice-start.6
  674.7 38.8 %copy-start.1 = (bf16[512,9,9,64]{0,3,2,1:T(8,128)(2,1)}, bf16[512,9,9,64]{0,3,2,1:T(8,128)(2,1)S(1)}, u32[]{:S(2)}) copy-start(bf16[512,9,9,64]{0,3,2,1:T(8,128)(2,1)S(1)} %get-tuple-element.182) | copy-start | bytes 15925252
  674.7 14.8 %slice-start = ((s8[13107200]{0:T(1024)(128)(4,1)}), s8[4194304]{0:T(1024)(128)(4,1)S(1)}, s32[]{:S(2)}) async-start(s8[13107200]{0:T(1024)(128)(4,1)} %bitcast.500), calls=%async_computation.2 | async-start | bytes 8388608
  674.7 14.8 %slice-start.1 = ((s8[13107200]{0:T(1024)(128)(4,1)}), s8[4194304]{0:T(1024)(128)(4,1)S(1)}, s32[]{:S(2)}) async-start(s8[13107200]{0:T(1024)(128)(4,1)} %bitcast.500), calls=%async_computation.3 | async-start | bytes 8388608
  682.9 6.6 slice-start.2
  682.9 6.6 slice-start.3
  819.6 15.6 %copy-start.7 = (f32[512,19]{1,0:T(8,128)S(1)}, f32[512,19]{1,0:T(8,128)}, u32[]{:S(2)}) copy-start(f32[512,19]{1,0:T(8,128)} %fusion.57) | copy-start | bytes 116740
  819.6 15.8 %copy-start.20 = (f32[1,64,64]{2,1,0:T(8,128)S(1)}, f32[1,64,64]{2,1,0:T(8,128)}, u32[]{:S(2)}) copy-start(f32[1,64,64]{2,1,0:T(8,128)} %convolution_bitcast_fusion.1) | copy-start | bytes 49156
  819.6 15.8 %copy-start.21 = (f32[1,64,64]{2,1,0:T(8,128)S(1)}, f32[1,64,64]{2,1,0:T(8,128)}, u32[]{:S(2)}) copy-start(f32[1,64,64]{2,1,0:T(8,128)} %convolution_bitcast_fusion.2) | copy-start | bytes 49156
  819.6 15.8 %copy-start.22 = (f32[1,64,64]{2,1,0:T(8,128)S(1)}, f32[1,64,64]{2,1,0:T(8,128)}, u32[]{:S(2)}) copy-start(f32[1,64,64]{2,1,0:T(8,128)} %convolution_bitcast_fusion.3) | copy-start | bytes 49156
  819.6 15.8 %copy-start.14 = (f32[1,64,64]{2,1,0:T(8,128)S(1)}, f32[1,64,64]{2,1,0:T(8,128)}, u32[]{:S(2)}) copy-start(f32[1,64,64]{2,1,0:T(8,128)} %convolution_bitcast_fusion.4) | copy-start | bytes 49156
  819.7 15.8 %copy-start.15 = (f32[1,64,64]{2,1,0:T(8,128)S(1)}, f32[1,64,64]{2,1,0:T(8,128)}, u32[]{:S(2)}) copy-start(f32[1,64,64]{2,1,0:T(8,128)} %convolution_bitcast_fusion.5) | copy-start | bytes 49156
  819.7 15.8 %copy-start.16 = (f32[1,64,64]{2,1,0:T(8,128)S(1)}, f32[1,64,64]{2,1,0:T(8,128)}, u32[]{:S(2)}) copy-start(f32[1,64,64]{2,1,0:T(8,128)} %convolution_bitcast_fusion.6) | copy-start | bytes 49156
  819.7 15.8 %copy-start.17 = (f32[1,64,64]{2,1,0:T(8,128)S(1)}, f32[1,64,64]{2,1,0:T(8,128)}, u32[]{:S(2)}) copy-start(f32[1,64,64]{2,1,0:T(8,128)} %convolution_bitcast_fusion.7) | copy-start | bytes 49156
  819.7 15.8 %copy-start.18 = (f32[1,64,64]{2,1,0:T(8,128)S(1)}, f32[1,64,64]{2,1,0:T(8,128)}, u32[]{:S(2)}) copy-start(f32[1,64,64]{2,1,0:T(8,128)} %convolution_bitcast_fusion.8) | copy-start | bytes 49156
  819.7 15.8 %copy-start.19 = (f32[1,64,64]{2,1,0:T(8,128)S(1)}, f32[1,64,64]{2,1,0:T(8,128)}, u32[]{:S(2)}) copy-start(f32[1,64,64]{2,1,0:T(8,128)} %convolution_bitcast_fusion.9) | copy-start | bytes 49156
  835.7 7.3 copy-start.11
  835.7 7.3 copy-start.12
  835.7 7.3 copy-start.13
  835.7 8.0 copy-start.32
  835.7 8.0 copy-start.38
  835.7 8.0 copy-start.40
  835.8 8.0 copy-start.42
  906.1 149.3 %copy-start.4 = (f32[105984]{0:T(1024)S(1)}, f32[105984]{0:T(1024)}, u32[]{:S(2)}) copy-start(f32[105984]{0:T(1024)} %param.23) | copy-start | bytes 1271812
  906.1 151.5 %copy-start.25 = (f32[1,4,128]{2,1,0:T(4,128)S(1)}, f32[1,4,128]{2,1,0:T(4,128)}, u32[]{:S(2)}) copy-start(f32[1,4,128]{2,1,0:T(4,128)} %param.18) | copy-start | bytes 6148
  906.1 151.5 %copy-start.28 = (f32[128,4]{0,1:T(4,128)S(1)}, f32[128,4]{0,1:T(4,128)}, u32[]{:S(2)}) copy-start(f32[128,4]{0,1:T(4,128)} %copy-done.26) | copy-start | bytes 6148
  906.1 151.5 %copy-start.31 = (f32[512]{0:T(512)S(1)}, f32[512]{0:T(512)}, u32[]{:S(2)}) copy-start(f32[512]{0:T(512)} %copy-done.30) | copy-start | bytes 6148
  906.1 151.5 %copy-start.33 = (f32[512]{0:T(512)S(1)}, f32[512]{0:T(512)}, u32[]{:S(2)}) copy-start(f32[512]{0:T(512)} %get-tuple-element.141) | copy-start | bytes 6148
  906.1 151.5 %copy-start.35 = (f32[1,4,128]{2,1,0:T(4,128)S(1)}, f32[1,4,128]{2,1,0:T(4,128)}, u32[]{:S(2)}) copy-start(f32[1,4,128]{2,1,0:T(4,128)} %param.22) | copy-start | bytes 6148
  906.1 151.5 %copy-start.36 = (f32[512,1]{0,1:T(1,128)S(1)}, f32[512,1]{0,1:T(1,128)}, u32[]{:S(2)}) copy-start(f32[512,1]{0,1:T(1,128)} %get-tuple-element.169) | copy-start | bytes 6148
  906.2 189.2 %all-reduce.21.cloned.1.call-start = ((), (), s32[]{:S(2)}) async-start(), calls=%async_computation.1 | async-start | bytes 851968 | tf_op jit(solution)/shard_map/psum | solution.py:275
  909.7 185.7 %copy-start.8 = (f32[105984]{0:T(1024)S(1)}, f32[105984]{0:T(1024)}, u32[]{:S(2)}) copy-start(f32[105984]{0:T(1024)} %param.26) | copy-start | bytes 1271812
  (10 other events, 19.7 us)
Sparse Core Ops, SparseCore 0:
  906.2 143.8 all-reduce.18
  1057.7 26.5 all-reduce.20
